TPU v7x, 32 devices: a whole 2x2x4 slice. The times are simulated.
32 devices in a mesh: dp: 8 (over z, x), tensor: 4 (over y, core).
Axes of the slice: x: 2, y: 2, z: 4, core: 2. Of those that a mesh axis runs over, the one named last changes fastest.
Arguments:
- layer_input: bfloat16 [32768, 1024], P(('dp', 'tensor')), may hold values from -6 to 6
- row_ids: int32 [32768], P('dp'), may hold values from 0 to 1, as said below
- input_gain: bfloat16 [1024], replicated, may hold values from 0.5 to 1.5
- input_shift: bfloat16 [1024], replicated, may hold values from -1.796875 to 1.796875
- query_weight: bfloat16 [1024, 1024], P(None, 'tensor'), may hold values from -0.1875 to 0.1875
- query_bias: bfloat16 [1024], P('tensor'), may hold values from -1.796875 to 1.796875
- key_weight: bfloat16 [1024, 1024], P(None, 'tensor'), may hold values from -0.1875 to 0.1875
- value_weight: bfloat16 [1024, 1024], P(None, 'tensor'), may hold values from -0.1875 to 0.1875
- value_bias: bfloat16 [1024], P('tensor'), may hold values from -1.796875 to 1.796875
- dense_weight: bfloat16 [1024, 1024], P('tensor'), may hold values from -0.75 to 0.75
- dense_bias: bfloat16 [1024], replicated, may hold values from -1.796875 to 1.796875
- post_gain: bfloat16 [1024], replicated, may hold values from 0.5 to 1.5
- post_shift: bfloat16 [1024], replicated, may hold values from -1.796875 to 1.796875
- up_weight: bfloat16 [1024, 4096], P(None, 'tensor'), may hold values from -0.1875 to 0.1875
- up_bias: bfloat16 [4096], P('tensor'), may hold values from -1.796875 to 1.796875
- down_weight: bfloat16 [4096, 1024], P('tensor'), may hold values from -0.1875 to 0.1875
- down_bias: bfloat16 [1024], replicated, may hold values from -1.796875 to 1.796875
- cotangent: bfloat16 [32768, 1024], P(('dp', 'tensor')), may hold values from -6 to 6
Outputs:
- layer_output: bfloat16 [32768, 1024], P(('dp', 'tensor'))
- input_grad: float32 [32768, 1024], P(('dp', 'tensor'))
- input_gain_grad: float32 [1024], replicated
- input_shift_grad: float32 [1024], replicated
- query_weight_grad: float32 [1024, 1024], P(None, 'tensor')
- query_bias_grad: float32 [1024], P('tensor')
- key_weight_grad: float32 [1024, 1024], P(None, 'tensor')
- value_weight_grad: float32 [1024, 1024], P(None, 'tensor')
- value_bias_grad: float32 [1024], P('tensor')
- dense_weight_grad: float32 [1024, 1024], P('tensor')
- dense_bias_grad: float32 [1024], replicated
- post_gain_grad: float32 [1024], replicated
- post_shift_grad: float32 [1024], replicated
- up_weight_grad: float32 [1024, 4096], P(None, 'tensor')
- up_bias_grad: float32 [4096], P('tensor')
- down_weight_grad: float32 [4096, 1024], P('tensor')
- down_bias_grad: float32 [1024], replicated
Inputs may be any that keep to these rules, and one draw needn't show every extreme that they name: `row_ids`: within each data group of 4096 consecutive tokens, the tokens form rows of 2048 or 4096 consecutive tokens, each row starting at a multiple of its own length within the group; every token of a row carries the index, within its group, of the row's last block of 2048 tokens, so ids never fall within a group and two rows of a group never share an id.
All inputs are finite; a program needn't handle non-finite values.
Results may differ from a plain program's by a relative error of at most 0.013.
Values may be sent and summed in bfloat16 or wider, within the bound.
A program may use at most 576 MiB of HBM per device.

v0:
```python
import jax
import jax.numpy as jnp
from jax import lax
from jax.sharding import PartitionSpec as P

HEADS = 16
HD = 64
SHORT = 2048
BLOCK = 512
EPSILON = 1e-05


def layer_norm(inputs, gain_vec, shift_vec):
    center = jnp.mean(inputs, axis=-1, keepdims=True)
    centered = inputs - center
    spread = jnp.mean(centered * centered, axis=-1, keepdims=True)
    return centered * lax.rsqrt(spread + EPSILON) * gain_vec + shift_vec


def gelu_tanh(inputs):
    return jax.nn.gelu(inputs, approximate=True)


def split_heads(matrix, head_count):
    return matrix.reshape(matrix.shape[0], head_count, HD).transpose(1, 0, 2)


def join_heads(stacked):
    return stacked.transpose(1, 0, 2).reshape(stacked.shape[1], stacked.shape[0] * stacked.shape[2])


def block_scores(query_block, key_block, slopes, query_first, key_first, query_ids, key_ids):
    products = jnp.einsum(
        "hqd,hkd->hqk", query_block, key_block, preferred_element_type=jnp.float32
    )
    query_pos = query_first + jnp.arange(query_block.shape[1])
    key_pos = key_first + jnp.arange(key_block.shape[1])
    offsets = (key_pos[None, :] - query_pos[:, None]).astype(jnp.float32)
    scores = products * HD ** (-0.5) + slopes[:, None, None] * offsets[None]
    allowed = (query_ids[:, None] == key_ids[None, :]) & (offsets <= 0)
    return jnp.where(allowed[None], scores, -1e30)


def shards(
    layer_input,
    row_ids,
    input_gain,
    input_shift,
    query_weight,
    query_bias,
    key_weight,
    value_weight,
    value_bias,
    dense_weight,
    dense_bias,
    post_gain,
    post_shift,
    up_weight,
    up_bias,
    down_weight,
    down_bias,
    cotangent,
):
    group_len = row_ids.shape[0]
    head_cols = query_weight.shape[1]
    head_count = head_cols // HD
    window_len = 2 * SHORT
    block_count = group_len // BLOCK

    def block_bounds(block_index):
        row_first = block_index * BLOCK
        key_first = row_first // window_len * window_len
        return (row_first, key_first, row_first + BLOCK)

    inputs = layer_input.astype(jnp.float32)
    normed, norm_pull = jax.vjp(
        layer_norm, inputs, input_gain.astype(jnp.float32), input_shift.astype(jnp.float32)
    )
    normed_low = normed.astype(jnp.bfloat16)
    normed_all = lax.all_gather(normed_low, "tensor", axis=0, tiled=True)
    joined = jnp.concatenate([query_weight, key_weight, value_weight], axis=1)
    projected = jnp.dot(normed_all, joined, preferred_element_type=jnp.float32)
    queries = (projected[:, :head_cols] + query_bias.astype(jnp.float32)).astype(jnp.bfloat16)
    key_rows = projected[:, head_cols : 2 * head_cols].astype(jnp.bfloat16)
    values = (projected[:, 2 * head_cols :] + value_bias.astype(jnp.float32)).astype(jnp.bfloat16)
    query_heads = split_heads(queries, head_count)
    key_heads = split_heads(key_rows, head_count)
    value_heads = split_heads(values, head_count)
    head_index = lax.axis_index("tensor") * head_count + jnp.arange(head_count)
    slopes = jnp.exp2(-8.0 * (head_index + 1).astype(jnp.float32) / HEADS)
    out_blocks = []
    total_blocks = []
    for block_index in range(block_count):
        row_first, key_first, row_last = block_bounds(block_index)
        masked = block_scores(
            query_heads[:, row_first:row_last],
            key_heads[:, key_first:row_last],
            slopes,
            row_first,
            key_first,
            row_ids[row_first:row_last],
            row_ids[key_first:row_last],
        )
        log_total = jax.nn.logsumexp(masked, axis=-1, keepdims=True)
        prob_low = jnp.exp(masked - log_total).astype(jnp.bfloat16)
        out_blocks.append(
            jnp.einsum(
                "hqk,hkd->hqd",
                prob_low,
                value_heads[:, key_first:row_last],
                preferred_element_type=jnp.float32,
            )
        )
        total_blocks.append(log_total)
    mixed_heads = join_heads(jnp.concatenate(out_blocks, axis=1)).astype(jnp.bfloat16)
    attended = lax.psum_scatter(
        jnp.dot(mixed_heads, dense_weight, preferred_element_type=jnp.float32),
        "tensor",
        scatter_dimension=0,
        tiled=True,
    )
    residual = inputs + attended + dense_bias.astype(jnp.float32)
    post_rows, post_pull = jax.vjp(
        layer_norm, residual, post_gain.astype(jnp.float32), post_shift.astype(jnp.float32)
    )
    post_low = post_rows.astype(jnp.bfloat16)
    post_all = lax.all_gather(post_low, "tensor", axis=0, tiled=True)
    hidden = jnp.dot(post_all, up_weight, preferred_element_type=jnp.float32) + up_bias.astype(
        jnp.float32
    )
    active, gelu_pull = jax.vjp(gelu_tanh, hidden)
    active_low = active.astype(jnp.bfloat16)
    ffn_out = lax.psum_scatter(
        jnp.dot(active_low, down_weight, preferred_element_type=jnp.float32),
        "tensor",
        scatter_dimension=0,
        tiled=True,
    )
    layer_output = (residual + ffn_out + down_bias.astype(jnp.float32)).astype(jnp.bfloat16)
    grad_rows = cotangent.astype(jnp.float32)
    down_bias_part = jnp.sum(grad_rows, axis=0)
    grad_all = lax.all_gather(cotangent, "tensor", axis=0, tiled=True)
    act_grad = jnp.einsum("td,fd->tf", grad_all, down_weight, preferred_element_type=jnp.float32)
    hidden_grad = gelu_pull(act_grad)[0].astype(jnp.bfloat16)
    up_part = jnp.einsum("td,tf->df", post_all, hidden_grad, preferred_element_type=jnp.float32)
    down_part = jnp.einsum("tf,td->fd", active_low, grad_all, preferred_element_type=jnp.float32)
    up_bias_part = jnp.sum(hidden_grad.astype(jnp.float32), axis=0)
    post_grad = lax.psum_scatter(
        jnp.einsum("tf,df->td", hidden_grad, up_weight, preferred_element_type=jnp.float32),
        "tensor",
        scatter_dimension=0,
        tiled=True,
    )
    norm_grad_resid, post_gain_part, post_shift_part = post_pull(post_grad)
    resid_grad = grad_rows + norm_grad_resid
    dense_bias_part = jnp.sum(resid_grad, axis=0)
    attended_all = lax.all_gather(resid_grad.astype(jnp.bfloat16), "tensor", axis=0, tiled=True)
    dense_part = jnp.einsum(
        "tc,td->cd", mixed_heads, attended_all, preferred_element_type=jnp.float32
    )
    mixed_grad = jnp.einsum(
        "td,cd->tc", attended_all, dense_weight, preferred_element_type=jnp.float32
    ).astype(jnp.bfloat16)
    grad_heads = split_heads(mixed_grad, head_count)
    query_grads = []
    key_acc = jnp.zeros((head_count, group_len, HD), jnp.float32)
    value_acc = jnp.zeros((head_count, group_len, HD), jnp.float32)
    for block_index in range(block_count):
        row_first, key_first, row_last = block_bounds(block_index)
        query_block = query_heads[:, row_first:row_last]
        key_block = key_heads[:, key_first:row_last]
        value_block = value_heads[:, key_first:row_last]
        out_grad = grad_heads[:, row_first:row_last]
        masked = block_scores(
            query_block,
            key_block,
            slopes,
            row_first,
            key_first,
            row_ids[row_first:row_last],
            row_ids[key_first:row_last],
        )
        prob_full = jnp.exp(masked - total_blocks[block_index])
        prob_low = prob_full.astype(jnp.bfloat16)
        value_acc = value_acc.at[:, key_first:row_last].add(
            jnp.einsum("hqk,hqd->hkd", prob_low, out_grad, preferred_element_type=jnp.float32)
        )
        prob_grad = jnp.einsum(
            "hqd,hkd->hqk", out_grad, value_block, preferred_element_type=jnp.float32
        )
        row_dot = jnp.sum(prob_full * prob_grad, axis=-1, keepdims=True)
        score_grad = (prob_full * (prob_grad - row_dot)).astype(jnp.bfloat16)
        query_grads.append(
            jnp.einsum("hqk,hkd->hqd", score_grad, key_block, preferred_element_type=jnp.float32)
            * HD ** (-0.5)
        )
        key_acc = key_acc.at[:, key_first:row_last].add(
            jnp.einsum("hqk,hqd->hkd", score_grad, query_block, preferred_element_type=jnp.float32)
            * HD ** (-0.5)
        )
    query_grad = join_heads(jnp.concatenate(query_grads, axis=1)).astype(jnp.bfloat16)
    key_grad = join_heads(key_acc).astype(jnp.bfloat16)
    value_grad = join_heads(value_acc).astype(jnp.bfloat16)
    proj_grad = jnp.concatenate([query_grad, key_grad, value_grad], axis=1)
    joined_part = jnp.einsum("td,tc->dc", normed_all, proj_grad, preferred_element_type=jnp.float32)
    query_bias_part = jnp.sum(query_grad.astype(jnp.float32), axis=0)
    value_bias_part = jnp.sum(value_grad.astype(jnp.float32), axis=0)
    normed_grad = lax.psum_scatter(
        jnp.einsum("tc,dc->td", proj_grad, joined, preferred_element_type=jnp.float32),
        "tensor",
        scatter_dimension=0,
        tiled=True,
    )
    input_norm_grad, input_gain_part, input_shift_part = norm_pull(normed_grad)
    input_grad = resid_grad + input_norm_grad
    summed = lax.psum(
        (
            joined_part[:, :head_cols],
            query_bias_part,
            joined_part[:, head_cols : 2 * head_cols],
            joined_part[:, 2 * head_cols :],
            value_bias_part,
            dense_part,
            up_part,
            up_bias_part,
            down_part,
        ),
        "dp",
    )
    shared = lax.psum(
        (
            input_gain_part,
            input_shift_part,
            dense_bias_part,
            post_gain_part,
            post_shift_part,
            down_bias_part,
        ),
        ("dp", "tensor"),
    )
    return (
        layer_output,
        input_grad,
        shared[0],
        shared[1],
        summed[0],
        summed[1],
        summed[2],
        summed[3],
        summed[4],
        summed[5],
        shared[2],
        shared[3],
        shared[4],
        summed[6],
        summed[7],
        summed[8],
        shared[5],
    )


def solution(mesh):
    in_specs = (
        P(("dp", "tensor"), None),
        P("dp"),
        P(),
        P(),
        P(None, "tensor"),
        P("tensor"),
        P(None, "tensor"),
        P(None, "tensor"),
        P("tensor"),
        P("tensor", None),
        P(),
        P(),
        P(),
        P(None, "tensor"),
        P("tensor"),
        P("tensor", None),
        P(),
        P(("dp", "tensor"), None),
    )
    out_specs = (
        P(("dp", "tensor"), None),
        P(("dp", "tensor"), None),
        P(),
        P(),
        P(None, "tensor"),
        P("tensor"),
        P(None, "tensor"),
        P(None, "tensor"),
        P("tensor"),
        P("tensor", None),
        P(),
        P(),
        P(),
        P(None, "tensor"),
        P("tensor"),
        P("tensor", None),
        P(),
    )
    return jax.shard_map(shards, mesh=mesh, in_specs=in_specs, out_specs=out_specs, check_vma=False)
```

profile of v0, /device:TPU:0, one launch (start us, length us, event | category | flops | bytes accessed | tf_op | source)
XLA Modules:
  0.0 1910.5 jit_solution(7665269605376054188)
XLA Ops:
  60.0 17.7 all-gather.5.cloned.1.call-done
  204.8 18.3 fusion.230
  223.2 16.4 exponential_reduce_fusion
  319.2 125.6 %reduce-scatter.5.cloned.1.call-done = f32[1024,1024]{1,0:T(8,128)} async-done(((f32[4096,1024]{1,0:T(8,128)}), f32[1024,1024]{1,0:T(8,128)}) %reduce-scatter.5.cloned.1.call-update) | async-done | bytes 4194320 | tf_op jit(solution)/shard_map/reduce_scatter | solution.py:116
  453.0 57.8 %all-gather.7.cloned.1.call-done = bf16[4096,1024]{1,0:T(8,128)(2,1)} async-done(((bf16[1024,1024]{1,0:T(8,128)(2,1)}), bf16[4096,1024]{1,0:T(8,128)(2,1)}) %all-gather.7.cloned.1.call-update) | async-done | bytes 8388624 | tf_op jit(solution)/shard_map/all_gather | solution.py:127
  510.8 16.1 fusion.233
  526.9 43.8 %all-gather.9.cloned.1.call-done = bf16[4096,1024]{1,0:T(8,128)(2,1)} async-done(((bf16[1024,1024]{1,0:T(8,128)(2,1)}), bf16[4096,1024]{1,0:T(8,128)(2,1)}) %all-gather.9.cloned.1.call-update) | async-done | bytes 8388624 | tf_op jit(solution)/shard_map/all_gather | solution.py:142
  570.6 27.1 %convert_reduce_fusion = (f32[1024]{0:T(1024)}, bf16[4096,1024]{1,0:T(8,128)(2,1)S(1)}, bf16[4096,1024]{1,0:T(8,128)(2,1)}) fusion(f32[4096,1024]{1,0:T(8,128)} %fusion.233, f32[1024]{0:T(1024)S(1)} %convert_element_type.310, bf16[4096,1024]{1,0:T(8,128)(2,1)} %all-gather.9.cloned.1.call-done, bf16[1024,1024]{1,0:T(8,128)(2,1)S(1)} %copy-done), kind=kOutput, calls=%fused_computation.32 | convolution fusion | flops 8694791168 | bytes 44048384 | tf_op jit(solution)/shard_map/td,fd->tf/dot_general | solution.py:143
  613.3 16.6 fusion.234
  630.6 109.0 %reduce-scatter.9.cloned.1.call-done = f32[1024,1024]{1,0:T(8,128)} async-done(((f32[4096,1024]{1,0:T(8,128)}), f32[1024,1024]{1,0:T(8,128)}) %reduce-scatter.9.cloned.1.call-update) | async-done | bytes 4194320 | tf_op jit(solution)/shard_map/reduce_scatter | solution.py:148
  744.4 123.7 %reduce-scatter.7.cloned.1.call-done = f32[1024,1024]{1,0:T(8,128)} async-done(((f32[4096,1024]{1,0:T(8,128)}), f32[1024,1024]{1,0:T(8,128)}) %reduce-scatter.7.cloned.1.call-update) | async-done | bytes 4194320 | tf_op jit(solution)/shard_map/reduce_scatter | solution.py:133
  878.7 58.4 %all-gather.11.cloned.1.call-done = bf16[4096,1024]{1,0:T(8,128)(2,1)} async-done(((bf16[1024,1024]{1,0:T(8,128)(2,1)}), bf16[4096,1024]{1,0:T(8,128)(2,1)}) %all-gather.11.cloned.1.call-update) | async-done | bytes 8388624 | tf_op jit(solution)/shard_map/all_gather | solution.py:157
  993.5 16.4 multiply_reduce_fusion.2
  1009.9 21.0 %multiply_reduce_fusion.1 = (f32[4,512]{1,0:T(4,128)}, f32[4,512,3584]{2,1,0:T(8,128)}) fusion(f32[4,512,3584]{2,1,0:T(8,128)} %get-tuple-element.284, f32[4,512]{1,0:T(4,128)S(1)} %copy-done.39, bf16[4,4096,64]{1,2,0:T(8,128)(2,1)S(1)} %bitcast.87, bf16[4,4096,64]{1,2,0:T(8,128)(2,1)} %bitcast.116), kind=kOutput, calls=%fused_computation.6 | convolution fusion | flops 961542144 | bytes 60833792 | tf_op jit(solution)/shard_map/hqd,hkd->hqk/dot_general | solution.py:188
  1030.9 22.6 %multiply_reduce_fusion = (f32[4,512]{1,0:T(4,128)}, f32[4,512,4096]{2,1,0:T(8,128)}) fusion(f32[4,512,4096]{2,1,0:T(8,128)} %get-tuple-element.286, f32[4,512]{1,0:T(4,128)S(1)} %copy-done.43, bf16[4,4096,64]{1,2,0:T(8,128)(2,1)S(1)} %bitcast.88, bf16[4,4096,64]{1,2,0:T(8,128)(2,1)S(1)} %bitcast.117), kind=kOutput, calls=%fused_computation.1 | convolution fusion | flops 1098905600 | bytes 69484544 | tf_op jit(solution)/shard_map/hqd,hkd->hqk/dot_general | solution.py:188
  1119.1 16.5 convert_reduce_fusion.3
  1218.0 16.8 multiply_convert_fusion.2
  1254.7 24.6 %multiply_convert_fusion.1 = bf16[4,512,3584]{2,1,0:T(8,128)(2,1)} fusion(f32[4,512,3584]{2,1,0:T(8,128)} %get-tuple-element.300, f32[4,512,3584]{2,1,0:T(8,128)} %get-tuple-element.284, f32[4,512]{1,0:T(4,128)S(1)} %copy-done.84, f32[4,512]{1,0:T(4,128)S(1)} %copy-done.39), kind=kLoop, calls=%fused_computation.5 | loop fusion | flops 29360128 | bytes 73416704 | tf_op jit(solution)/shard_map/convert_element_type | solution.py:192
  1295.8 27.6 %multiply_convert_fusion = bf16[4,512,4096]{2,1,0:T(8,128)(2,1)} fusion(f32[4,512,4096]{2,1,0:T(8,128)} %get-tuple-element.302, f32[4,512,4096]{2,1,0:T(8,128)} %get-tuple-element.286, f32[4,512]{1,0:T(4,128)S(1)} %copy-done.83, f32[4,512]{1,0:T(4,128)S(1)} %copy-done.43), kind=kLoop, calls=%fused_computation | loop fusion | flops 33554432 | bytes 83902464 | tf_op jit(solution)/shard_map/convert_element_type | solution.py:192
  1370.4 18.2 fusion.237
  1407.5 22.4 %all-reduce.3 = (f32[256]{0:T(256)}, f32[256]{0:T(256)}, f32[1024]{0:T(1024)}) all-reduce(f32[256]{0:T(256)S(1)} %reduce_sum.360, f32[256]{0:T(256)S(1)} %reduce_sum.362, f32[1024]{0:T(1024)S(1)} %copy-done.92), channel_id=1, replica_groups=mesh['dp'=8,'tensor'=4] {'dp'}, use_global_device_ids=true, to_apply=%region_42.43 | all-reduce | flops 1536 | bytes 12288 | tf_op jit(solution)/shard_map/psum | solution.py:216
  1429.9 51.0 %reduce-scatter.11.cloned.1.call-done = f32[1024,1024]{1,0:T(8,128)} async-done(((f32[4096,1024]{1,0:T(8,128)}), f32[1024,1024]{1,0:T(8,128)}) %reduce-scatter.11.cloned.1.call-update) | async-done | bytes 4194320 | tf_op jit(solution)/shard_map/reduce_scatter | solution.py:208
  1490.8 44.6 %all-reduce.2 = (f32[1024]{0:T(1024)}, f32[1024]{0:T(1024)}, f32[1024]{0:T(1024)}, f32[1024]{0:T(1024)}, f32[1024]{0:T(1024)}, /*index=5*/f32[1024]{0:T(1024)}) all-reduce(f32[1024]{0:T(1024)S(1)} %get-tuple-element.227, f32[1024]{0:T(1024)S(1)} %get-tuple-element.230, ...), channel_id=1, replica_groups=mesh['dp'=8,'tensor'=4] {'dp','tensor'}, use_global_device_ids=true, to_apply=%region_37.38 | all-reduce | flops 6144 | bytes 49152 | tf_op jit(solution)/shard_map/psum | solution.py:230
  1535.4 355.9 %all-reduce.7.cloned.1.call-done = (f32[1024,256]{1,0:T(8,128)}, f32[1024,256]{1,0:T(8,128)}, f32[1024,256]{1,0:T(8,128)}, f32[256,1024]{1,0:T(8,128)}, f32[1024,1024]{1,0:T(8,128)}, /*index=5*/f32[1024,1024]{1,0:T(8,128)}) async-done(((f32[1024,256]{1,0:T(8,128)}, f32[1024,256]{1,0:T(8,128)}, f32[1024,256]{1,0:T(8,128)}, f32[256,1024]{1,0:T(8,128)}, f32[1024,1024]{1,0:T(8,128)}, ...) | async-done | bytes 12582928 | tf_op jit(solution)/shard_map/psum | solution.py:216
  (422 shorter events, 627.4 us)
Async XLA Ops:
  7.2 563.4 %copy-start = (bf16[1024,1024]{1,0:T(8,128)(2,1)S(1)}, bf16[1024,1024]{1,0:T(8,128)(2,1)}, u32[]{:S(2)}) copy-start(bf16[1024,1024]{1,0:T(8,128)(2,1)} %param.69) | copy-start | bytes 6291460
  7.2 70.5 %all-gather.5.cloned.1.call-start = ((), (), s32[]{:S(2)}) async-start(), calls=%async_computation.4 | async-start | bytes 10485760 | tf_op jit(solution)/shard_map/all_gather | solution.py:80
  16.6 428.2 %reduce-scatter.5.cloned.1.call-start = ((), (), s32[]{:S(2)}) async-start(), calls=%async_computation.5 | async-start | bytes 20971520 | tf_op jit(solution)/shard_map/reduce_scatter | solution.py:116
  94.4 145.1 %copy-start.66 = (f32[4,512]{1,0:T(4,128)}, f32[4,512]{1,0:T(4,128)S(1)}, u32[]{:S(2)}) copy-start(f32[4,512]{1,0:T(4,128)S(1)} %log_add_fusion.7) | copy-start | bytes 24580
  102.0 139.1 %copy-start.63 = (f32[4,512]{1,0:T(4,128)}, f32[4,512]{1,0:T(4,128)S(1)}, u32[]{:S(2)}) copy-start(f32[4,512]{1,0:T(4,128)S(1)} %log_add_fusion.6) | copy-start | bytes 24580
  110.2 133.3 %copy-start.59 = (f32[4,512]{1,0:T(4,128)}, f32[4,512]{1,0:T(4,128)S(1)}, u32[]{:S(2)}) copy-start(f32[4,512]{1,0:T(4,128)S(1)} %log_add_fusion.5) | copy-start | bytes 24580
  128.6 122.2 %copy-start.68 = (f32[4,512]{1,0:T(4,128)}, f32[4,512]{1,0:T(4,128)S(1)}, u32[]{:S(2)}) copy-start(f32[4,512]{1,0:T(4,128)S(1)} %log_add_fusion.4) | copy-start | bytes 24580
  151.3 109.0 %copy-start.51 = (f32[4,512]{1,0:T(4,128)}, f32[4,512]{1,0:T(4,128)S(1)}, u32[]{:S(2)}) copy-start(f32[4,512]{1,0:T(4,128)S(1)} %log_add_fusion.3) | copy-start | bytes 24580
  175.8 94.6 %copy-start.40 = (f32[4,512]{1,0:T(4,128)}, f32[4,512]{1,0:T(4,128)S(1)}, u32[]{:S(2)}) copy-start(f32[4,512]{1,0:T(4,128)S(1)} %log_add_fusion.2) | copy-start | bytes 24580
  204.8 76.6 %copy-start.38 = (f32[4,512]{1,0:T(4,128)}, f32[4,512]{1,0:T(4,128)S(1)}, u32[]{:S(2)}) copy-start(f32[4,512]{1,0:T(4,128)S(1)} %log_add_fusion.1) | copy-start | bytes 24580
  318.5 192.3 %all-gather.7.cloned.1.call-start = ((), (), s32[]{:S(2)}) async-start(), calls=%async_computation.6 | async-start | bytes 10485760 | tf_op jit(solution)/shard_map/all_gather | solution.py:127
  452.3 118.3 %all-gather.9.cloned.1.call-start = ((), (), s32[]{:S(2)}) async-start(), calls=%async_computation.8 | async-start | bytes 10485760 | tf_op jit(solution)/shard_map/all_gather | solution.py:142
  452.9 286.6 %reduce-scatter.9.cloned.1.call-start = ((), (), s32[]{:S(2)}) async-start(), calls=%async_computation.9 | async-start | bytes 20971520 | tf_op jit(solution)/shard_map/reduce_scatter | solution.py:148
  613.2 254.9 %reduce-scatter.7.cloned.1.call-start = ((), (), s32[]{:S(2)}) async-start(), calls=%async_computation.7 | async-start | bytes 20971520 | tf_op jit(solution)/shard_map/reduce_scatter | solution.py:133
  629.9 307.2 %all-gather.11.cloned.1.call-start = ((), (), s32[]{:S(2)}) async-start(), calls=%async_computation.10 | async-start | bytes 10485760 | tf_op jit(solution)/shard_map/all_gather | solution.py:157
  744.4 132.3 %copy-start.24 = (bf16[1024,1024]{1,0:T(8,128)(2,1)S(1)}, bf16[1024,1024]{1,0:T(8,128)(2,1)}, u32[]{:S(2)}) copy-start(bf16[1024,1024]{1,0:T(8,128)(2,1)} %param.71) | copy-start | bytes 6291460
  878.7 64.4 %copy-start.67 = (f32[4,512]{1,0:T(4,128)S(1)}, f32[4,512]{1,0:T(4,128)}, u32[]{:S(2)}) copy-start(f32[4,512]{1,0:T(4,128)} %copy-done.66) | copy-start | bytes 24580
  878.7 602.2 %reduce-scatter.11.cloned.1.call-start = ((), (), s32[]{:S(2)}) async-start(), calls=%async_computation.11 | async-start | bytes 20971520 | tf_op jit(solution)/shard_map/reduce_scatter | solution.py:208
  1354.6 536.7 %all-reduce.7.cloned.1.call-start = ((), (), s32[]{:S(2)}) async-start(), calls=%async_computation.12 | async-start | bytes 25165824 | tf_op jit(solution)/shard_map/psum | solution.py:216
  1404.7 76.2 %copy-start.14 = (bf16[1024,1024]{1,0:T(8,128)(2,1)S(1)}, bf16[1024,1024]{1,0:T(8,128)(2,1)}, u32[]{:S(2)}) copy-start(bf16[1024,1024]{1,0:T(8,128)(2,1)} %param.54) | copy-start | bytes 6291460
  1404.7 76.2 %copy-start.73 = (f32[1024]{0:T(1024)S(1)}, f32[1024]{0:T(1024)}, u32[]{:S(2)}) copy-start(f32[1024]{0:T(1024)} %copy-done.72) | copy-start | bytes 12292
  1404.7 76.2 %copy-start.75 = (f32[1024]{0:T(1024)S(1)}, f32[1024]{0:T(1024)}, u32[]{:S(2)}) copy-start(f32[1024]{0:T(1024)} %copy-done.74) | copy-start | bytes 12292
  1405.4 78.8 %copy-start.79 = (f32[1024]{0:T(1024)S(1)}, f32[1024]{0:T(1024)}, u32[]{:S(2)}) copy-start(f32[1024]{0:T(1024)} %copy-done.78) | copy-start | bytes 12292
  1405.4 78.9 %copy-start.77 = (f32[1024]{0:T(1024)S(1)}, f32[1024]{0:T(1024)}, u32[]{:S(2)}) copy-start(f32[1024]{0:T(1024)} %copy-done.76) | copy-start | bytes 12292
  (109 other events, 923.8 us)
Sparse Core Ops, SparseCore 0:
  16.7 60.9 all-gather.4
  318.6 126.0 reduce-scatter.4
  452.5 58.2 all-gather.6
  512.3 58.2 all-gather.8
  613.3 126.1 reduce-scatter.8
  741.9 126.1 reduce-scatter.6
  878.8 58.2 all-gather.10
  1354.7 126.0 reduce-scatter.10
  1487.4 403.8 all-reduce.6
where the time goes:
time: 1920 us; the launch traced here: 1910 us
  waiting for transfers between devices  943 us (49%)
  matrix products  579 us (30%)
  other arithmetic  253 us (13%)
  blocking collectives  67 us (3%)
  local copies, waits for them, and re-layouts  52.7 us (3%)
    psum x1, waiting for transfers between devices, shards(): lax.psum((joined_part[:, :head_cols], query_bias_part, joined_part[:, hea...  356 us
    reduce_scatter x1, waiting for transfers between devices, shards(): lax.psum_scatter(jnp.dot(mixed_heads, dense_weight, preferred_element_typ...  126 us
    reduce_scatter x1, waiting for transfers between devices, shards(): lax.psum_scatter(jnp.dot(active_low, down_weight, preferred_element_type=...  124 us
    reduce_scatter x1, waiting for transfers between devices, shards(): lax.psum_scatter(jnp.einsum('tf,df->td', hidden_grad, up_weight, preferre...  109 us
    convert_element_type x8, other arithmetic, shards(): score_grad = (prob_full * (prob_grad - row_dot)).astype(jnp.bfloat16)  107 us
    dot_general x8, matrix products, shards(): jnp.einsum('hqd,hkd->hqk', out_grad, value_block, preferred_element_type=...  102 us
    dot_general x8, matrix products, shards(): jnp.einsum('hqk,hqd->hkd', prob_low, out_grad, preferred_element_type=jnp...  80.3 us
    dot_general x8, matrix products, block_scores(): jnp.einsum('hqd,hkd->hqk', query_block, key_block, preferred_element_type...  78.1 us
  transfers between devices with their start and end apart: 9, of which 9 were waited for; matrix products, arithmetic and copies ran while one was open for 7% of the time, Pallas kernels for 0%

commit v1 on v0

--- a/solution.py
+++ b/solution.py
@@ -124,7 +124,14 @@
         layer_norm, residual, post_gain.astype(jnp.float32), post_shift.astype(jnp.float32)
     )
     post_low = post_rows.astype(jnp.bfloat16)
-    post_all = lax.all_gather(post_low, "tensor", axis=0, tiled=True)
+    ring = [post_low]
+    for hop in range(3):
+        ring.append(lax.ppermute(ring[-1], "tensor", [(dev, (dev + 1) % 4) for dev in range(4)]))
+    post_all = jnp.roll(
+        jnp.concatenate(ring[::-1], axis=0),
+        (lax.axis_index("tensor") + 1) * ring[0].shape[0],
+        axis=0,
+    )
     hidden = jnp.dot(post_all, up_weight, preferred_element_type=jnp.float32) + up_bias.astype(
         jnp.float32
     )

time: 1920 us -> 1930 us (level)
    ppermute x0 -> x3, waiting for transfers between devices: none -> 101 us  [shards(): lax.ppermute(ring[-1], 'tensor', [(dev, (dev + 1) % 4) for dev in range(4)])]
    all_gather x1 -> x0, waiting for transfers between devices: 57.8 us -> none  [shards(): post_all = lax.all_gather(post_low, 'tensor', axis=0, tiled=True)]
    all_gather x1, waiting for transfers between devices: 43.8 us -> 0.02 us  [shards(): grad_all = lax.all_gather(cotangent, 'tensor', axis=0, tiled=True)]
    unnamed x246 -> x258, local copies, waits for them, and re-layouts: 44.4 us -> 61.5 us
  transfers between devices with their start and end apart: 9 -> 11, of which waited for: 9 -> 10; matrix products, arithmetic and copies ran while one was open for 7% -> 8% of each run, Pallas kernels for 0% -> 0%
where the time goes in v1:
time: 1930 us
  waiting for transfers between devices  941 us (49%)
  matrix products  578 us (30%)
  other arithmetic  256 us (13%)
  local copies, waits for them, and re-layouts  69.8 us (4%)
  blocking collectives  67 us (3%)
    psum x1, waiting for transfers between devices, shards(): lax.psum((joined_part[:, :head_cols], query_bias_part, joined_part[:, hea...  356 us
    reduce_scatter x1, waiting for transfers between devices, shards(): lax.psum_scatter(jnp.dot(mixed_heads, dense_weight, preferred_element_typ...  125 us
    reduce_scatter x1, waiting for transfers between devices, shards(): lax.psum_scatter(jnp.dot(active_low, down_weight, preferred_element_type=...  124 us
    reduce_scatter x1, waiting for transfers between devices, shards(): lax.psum_scatter(jnp.einsum('tf,df->td', hidden_grad, up_weight, preferre...  107 us
    convert_element_type x8, other arithmetic, shards(): score_grad = (prob_full * (prob_grad - row_dot)).astype(jnp.bfloat16)  107 us
    dot_general x8, matrix products, shards(): jnp.einsum('hqd,hkd->hqk', out_grad, value_block, preferred_element_type=...  101 us
    ppermute x3, waiting for transfers between devices, shards(): lax.ppermute(ring[-1], 'tensor', [(dev, (dev + 1) % 4) for dev in range(4)])  101 us
    dot_general x8, matrix products, shards(): jnp.einsum('hqk,hqd->hkd', prob_low, out_grad, preferred_element_type=jnp...  80.3 us
  transfers between devices with their start and end apart: 11, of which 10 were waited for; matrix products, arithmetic and copies ran while one was open for 8% of the time, Pallas kernels for 0%

profile of v1, /device:TPU:0, one launch (start us, length us, event | category | flops | bytes accessed | tf_op | source)
XLA Modules:
  0.0 1928.7 jit_solution(2734707135812770526)
XLA Ops:
  60.1 17.6 all-gather.4.cloned.1.call-done
  204.9 18.2 fusion.236
  223.1 16.4 exponential_reduce_fusion
  319.3 125.5 %reduce-scatter.5.cloned.1.call-done = f32[1024,1024]{1,0:T(8,128)} async-done(((f32[4096,1024]{1,0:T(8,128)}), f32[1024,1024]{1,0:T(8,128)}) %reduce-scatter.5.cloned.1.call-update) | async-done | bytes 4194320 | tf_op jit(solution)/shard_map/reduce_scatter | solution.py:116
  450.7 61.6 %collective-permute-done = bf16[1024,1024]{1,0:T(8,128)(2,1)S(1)} collective-permute-done((bf16[1024,1024]{1,0:T(8,128)(2,1)S(1)}, bf16[1024,1024]{1,0:T(8,128)(2,1)S(1)}, u32[]{:S(2)}, u32[]{:S(2)}) %collective-permute-start) | collective-permute-done | bytes 2097184 | tf_op jit(solution)/shard_map/ppermute | solution.py:129
  513.6 30.1 %collective-permute-done.1 = bf16[1024,1024]{1,0:T(8,128)(2,1)} collective-permute-done((bf16[1024,1024]{1,0:T(8,128)(2,1)S(1)}, bf16[1024,1024]{1,0:T(8,128)(2,1)}, u32[]{:S(2)}, u32[]{:S(2)}) %collective-permute-start.1) | collective-permute-done | bytes 2097184 | tf_op jit(solution)/shard_map/ppermute | solution.py:129
  543.7 16.2 fusion.240
  589.1 26.7 %convert_reduce_fusion = (f32[1024]{0:T(1024)}, bf16[4096,1024]{1,0:T(8,128)(2,1)S(1)}, bf16[4096,1024]{1,0:T(8,128)(2,1)}) fusion(f32[4096,1024]{1,0:T(8,128)} %fusion.240, f32[1024]{0:T(1024)S(1)} %convert_element_type.310, bf16[1024,1024]{1,0:T(8,128)(2,1)S(1)} %copy-done, bf16[8192,1024]{1,0:T(8,128)(2,1)} %constant_dynamic-update-slice_fusion.3, ...), kind=kOutput, calls=%fused_computation.32 | convolution fusion | flops 8694791168 | bytes 44048388 | tf_op jit(solution)/shard_map/dot_general | solution.py:135
  632.7 16.8 fusion.239
  650.2 107.2 %reduce-scatter.9.cloned.1.call-done = f32[1024,1024]{1,0:T(8,128)} async-done(((f32[4096,1024]{1,0:T(8,128)}), f32[1024,1024]{1,0:T(8,128)}) %reduce-scatter.9.cloned.1.call-update) | async-done | bytes 4194320 | tf_op jit(solution)/shard_map/reduce_scatter | solution.py:155
  762.3 123.7 %reduce-scatter.7.cloned.1.call-done = f32[1024,1024]{1,0:T(8,128)} async-done(((f32[4096,1024]{1,0:T(8,128)}), f32[1024,1024]{1,0:T(8,128)}) %reduce-scatter.7.cloned.1.call-update) | async-done | bytes 4194320 | tf_op jit(solution)/shard_map/reduce_scatter | solution.py:140
  896.6 58.4 %all-gather.8.cloned.1.call-done = bf16[4096,1024]{1,0:T(8,128)(2,1)} async-done(((bf16[1024,1024]{1,0:T(8,128)(2,1)}), bf16[4096,1024]{1,0:T(8,128)(2,1)}) %all-gather.8.cloned.1.call-update) | async-done | bytes 8388624 | tf_op jit(solution)/shard_map/all_gather | solution.py:164
  1011.2 16.3 multiply_reduce_fusion.2
  1027.6 21.0 %multiply_reduce_fusion.1 = (f32[4,512]{1,0:T(4,128)}, f32[4,512,3584]{2,1,0:T(8,128)}) fusion(f32[4,512,3584]{2,1,0:T(8,128)} %get-tuple-element.284, f32[4,512]{1,0:T(4,128)S(1)} %copy-done.42, bf16[4,4096,64]{1,2,0:T(8,128)(2,1)S(1)} %bitcast.85, bf16[4,4096,64]{1,2,0:T(8,128)(2,1)} %bitcast.114), kind=kOutput, calls=%fused_computation.6 | convolution fusion | flops 961542144 | bytes 60833792 | tf_op jit(solution)/shard_map/hqd,hkd->hqk/dot_general | solution.py:195
  1048.6 22.6 %multiply_reduce_fusion = (f32[4,512]{1,0:T(4,128)}, f32[4,512,4096]{2,1,0:T(8,128)}) fusion(f32[4,512,4096]{2,1,0:T(8,128)} %get-tuple-element.286, f32[4,512]{1,0:T(4,128)S(1)} %copy-done.46, bf16[4,4096,64]{1,2,0:T(8,128)(2,1)S(1)} %bitcast.86, bf16[4,4096,64]{1,2,0:T(8,128)(2,1)S(1)} %bitcast.115), kind=kOutput, calls=%fused_computation.1 | convolution fusion | flops 1098905600 | bytes 69484544 | tf_op jit(solution)/shard_map/hqd,hkd->hqk/dot_general | solution.py:195
  1136.8 16.4 convert_reduce_fusion.3
  1235.8 16.8 multiply_convert_fusion.2
  1272.4 24.6 %multiply_convert_fusion.1 = bf16[4,512,3584]{2,1,0:T(8,128)(2,1)} fusion(f32[4,512,3584]{2,1,0:T(8,128)} %get-tuple-element.300, f32[4,512,3584]{2,1,0:T(8,128)} %get-tuple-element.284, f32[4,512]{1,0:T(4,128)S(1)} %copy-done.87, f32[4,512]{1,0:T(4,128)S(1)} %copy-done.42), kind=kLoop, calls=%fused_computation.5 | loop fusion | flops 29360128 | bytes 73416704 | tf_op jit(solution)/shard_map/convert_element_type | solution.py:199
  1313.7 27.6 %multiply_convert_fusion = bf16[4,512,4096]{2,1,0:T(8,128)(2,1)} fusion(f32[4,512,4096]{2,1,0:T(8,128)} %get-tuple-element.302, f32[4,512,4096]{2,1,0:T(8,128)} %get-tuple-element.286, f32[4,512]{1,0:T(4,128)S(1)} %copy-done.86, f32[4,512]{1,0:T(4,128)S(1)} %copy-done.46), kind=kLoop, calls=%fused_computation | loop fusion | flops 33554432 | bytes 83902464 | tf_op jit(solution)/shard_map/convert_element_type | solution.py:199
  1388.3 18.2 fusion.13
  1425.3 22.5 %all-reduce.3 = (f32[256]{0:T(256)}, f32[256]{0:T(256)}, f32[1024]{0:T(1024)}) all-reduce(f32[256]{0:T(256)S(1)} %reduce_sum.360, f32[256]{0:T(256)S(1)} %reduce_sum.362, f32[1024]{0:T(1024)S(1)} %copy-done.95), channel_id=1, replica_groups=mesh['dp'=8,'tensor'=4] {'dp'}, use_global_device_ids=true, to_apply=%region_42.43 | all-reduce | flops 1536 | bytes 12288 | tf_op jit(solution)/shard_map/psum | solution.py:223
  1447.7 51.1 %reduce-scatter.11.cloned.1.call-done = f32[1024,1024]{1,0:T(8,128)} async-done(((f32[4096,1024]{1,0:T(8,128)}), f32[1024,1024]{1,0:T(8,128)}) %reduce-scatter.11.cloned.1.call-update) | async-done | bytes 4194320 | tf_op jit(solution)/shard_map/reduce_scatter | solution.py:215
  1508.7 44.6 %all-reduce.2 = (f32[1024]{0:T(1024)}, f32[1024]{0:T(1024)}, f32[1024]{0:T(1024)}, f32[1024]{0:T(1024)}, f32[1024]{0:T(1024)}, /*index=5*/f32[1024]{0:T(1024)}) all-reduce(f32[1024]{0:T(1024)S(1)} %get-tuple-element.227, f32[1024]{0:T(1024)S(1)} %get-tuple-element.230, ...), channel_id=1, replica_groups=mesh['dp'=8,'tensor'=4] {'dp','tensor'}, use_global_device_ids=true, to_apply=%region_37.38 | all-reduce | flops 6144 | bytes 49152 | tf_op jit(solution)/shard_map/psum | solution.py:237
  1553.3 355.9 %all-reduce.7.cloned.1.call-done = (f32[1024,256]{1,0:T(8,128)}, f32[1024,256]{1,0:T(8,128)}, f32[1024,256]{1,0:T(8,128)}, f32[256,1024]{1,0:T(8,128)}, f32[1024,1024]{1,0:T(8,128)}, /*index=5*/f32[1024,1024]{1,0:T(8,128)}) async-done(((f32[1024,256]{1,0:T(8,128)}, f32[1024,256]{1,0:T(8,128)}, f32[1024,256]{1,0:T(8,128)}, f32[256,1024]{1,0:T(8,128)}, f32[1024,1024]{1,0:T(8,128)}, ...) | async-done | bytes 12582928 | tf_op jit(solution)/shard_map/psum | solution.py:223
  (439 shorter events, 657.2 us)
Async XLA Ops:
  7.2 581.9 %copy-start = (bf16[1024,1024]{1,0:T(8,128)(2,1)S(1)}, bf16[1024,1024]{1,0:T(8,128)(2,1)}, u32[]{:S(2)}) copy-start(bf16[1024,1024]{1,0:T(8,128)(2,1)} %param.67) | copy-start | bytes 6291460
  7.2 70.5 %all-gather.4.cloned.1.call-start = ((), (), s32[]{:S(2)}) async-start(), calls=%async_computation.4 | async-start | bytes 10485760 | tf_op jit(solution)/shard_map/all_gather | solution.py:80
  16.6 428.2 %reduce-scatter.5.cloned.1.call-start = ((), (), s32[]{:S(2)}) async-start(), calls=%async_computation.5 | async-start | bytes 20971520 | tf_op jit(solution)/shard_map/reduce_scatter | solution.py:116
  94.4 145.1 %copy-start.69 = (f32[4,512]{1,0:T(4,128)}, f32[4,512]{1,0:T(4,128)S(1)}, u32[]{:S(2)}) copy-start(f32[4,512]{1,0:T(4,128)S(1)} %log_add_fusion.7) | copy-start | bytes 24580
  102.0 139.0 %copy-start.66 = (f32[4,512]{1,0:T(4,128)}, f32[4,512]{1,0:T(4,128)S(1)}, u32[]{:S(2)}) copy-start(f32[4,512]{1,0:T(4,128)S(1)} %log_add_fusion.6) | copy-start | bytes 24580
  110.3 133.1 %copy-start.62 = (f32[4,512]{1,0:T(4,128)}, f32[4,512]{1,0:T(4,128)S(1)}, u32[]{:S(2)}) copy-start(f32[4,512]{1,0:T(4,128)S(1)} %log_add_fusion.5) | copy-start | bytes 24580
  128.6 122.2 %copy-start.71 = (f32[4,512]{1,0:T(4,128)}, f32[4,512]{1,0:T(4,128)S(1)}, u32[]{:S(2)}) copy-start(f32[4,512]{1,0:T(4,128)S(1)} %log_add_fusion.4) | copy-start | bytes 24580
  151.3 109.0 %copy-start.54 = (f32[4,512]{1,0:T(4,128)}, f32[4,512]{1,0:T(4,128)S(1)}, u32[]{:S(2)}) copy-start(f32[4,512]{1,0:T(4,128)S(1)} %log_add_fusion.3) | copy-start | bytes 24580
  175.9 94.5 %copy-start.43 = (f32[4,512]{1,0:T(4,128)}, f32[4,512]{1,0:T(4,128)S(1)}, u32[]{:S(2)}) copy-start(f32[4,512]{1,0:T(4,128)S(1)} %log_add_fusion.2) | copy-start | bytes 24580
  204.9 76.5 %copy-start.41 = (f32[4,512]{1,0:T(4,128)}, f32[4,512]{1,0:T(4,128)S(1)}, u32[]{:S(2)}) copy-start(f32[4,512]{1,0:T(4,128)S(1)} %log_add_fusion.1) | copy-start | bytes 24580
  318.5 225.2 %all-gather.6.cloned.1.call-start = ((), (), s32[]{:S(2)}) async-start(), calls=%async_computation.7 | async-start | bytes 10485760 | tf_op jit(solution)/shard_map/all_gather | solution.py:149
  319.2 438.2 %reduce-scatter.9.cloned.1.call-start = ((), (), s32[]{:S(2)}) async-start(), calls=%async_computation.8 | async-start | bytes 20971520 | tf_op jit(solution)/shard_map/reduce_scatter | solution.py:155
  448.9 94.8 %copy-start.99 = (bf16[1024]{0:T(1024)(128)(2,1)S(1)}, bf16[1024]{0:T(1024)(128)(2,1)}, u32[]{:S(2)}) copy-start(bf16[1024]{0:T(1024)(128)(2,1)} %param.68) | copy-start | bytes 6148
  450.3 62.0 %collective-permute-start = (bf16[1024,1024]{1,0:T(8,128)(2,1)S(1)}, bf16[1024,1024]{1,0:T(8,128)(2,1)S(1)}, u32[]{:S(2)}, u32[]{:S(2)}) collective-permute-start(bf16[1024,1024]{1,0:T(8,128)(2,1)S(1)} %add_convert_fusion.1), channel_id=1, source_target_pairs={{0,1},{1,2},{2,3},{3,0},{4,5},{5,6},{6,7},{7,4},{8,9},{9,10},{10,1... | collective-permute-start | bytes 6291464 | tf_op jit(solution)/shard_map/ppermute | solution.py:129
  513.6 30.1 %collective-permute-start.1 = (bf16[1024,1024]{1,0:T(8,128)(2,1)S(1)}, bf16[1024,1024]{1,0:T(8,128)(2,1)}, u32[]{:S(2)}, u32[]{:S(2)}) collective-permute-start(bf16[1024,1024]{1,0:T(8,128)(2,1)S(1)} %collective-permute-done), channel_id=1, source_target_pairs={{0,1},{1,2},{2,3},{3,0},{4,5},{5,6},{6,7},{7,4},{8,9},{9,10},{10,1... | collective-permute-start | bytes 6291464 | tf_op jit(solution)/shard_map/ppermute | solution.py:129
  543.7 25.8 %collective-permute-start.2 = (bf16[1024,1024]{1,0:T(8,128)(2,1)}, bf16[1024,1024]{1,0:T(8,128)(2,1)}, u32[]{:S(2)}, u32[]{:S(2)}) collective-permute-start(bf16[1024,1024]{1,0:T(8,128)(2,1)} %collective-permute-done.1), channel_id=1, source_target_pairs={{0,1},{1,2},{2,3},{3,0},{4,5},{5,6},{6,7},{7,4},{8,9},{9,10},{10,1... | collective-permute-start | bytes 6291464 | tf_op jit(solution)/shard_map/ppermute | solution.py:129
  631.1 254.9 %reduce-scatter.7.cloned.1.call-start = ((), (), s32[]{:S(2)}) async-start(), calls=%async_computation.6 | async-start | bytes 20971520 | tf_op jit(solution)/shard_map/reduce_scatter | solution.py:140
  649.6 305.5 %all-gather.8.cloned.1.call-start = ((), (), s32[]{:S(2)}) async-start(), calls=%async_computation.9 | async-start | bytes 10485760 | tf_op jit(solution)/shard_map/all_gather | solution.py:164
  762.3 132.3 %copy-start.25 = (bf16[1024,1024]{1,0:T(8,128)(2,1)S(1)}, bf16[1024,1024]{1,0:T(8,128)(2,1)}, u32[]{:S(2)}) copy-start(bf16[1024,1024]{1,0:T(8,128)(2,1)} %param.71) | copy-start | bytes 6291460
  896.6 602.2 %reduce-scatter.11.cloned.1.call-start = ((), (), s32[]{:S(2)}) async-start(), calls=%async_computation.10 | async-start | bytes 20971520 | tf_op jit(solution)/shard_map/reduce_scatter | solution.py:215
  1372.5 536.7 %all-reduce.7.cloned.1.call-start = ((), (), s32[]{:S(2)}) async-start(), calls=%async_computation.11 | async-start | bytes 25165824 | tf_op jit(solution)/shard_map/psum | solution.py:223
  1422.5 76.3 %copy-start.76 = (f32[1024]{0:T(1024)S(1)}, f32[1024]{0:T(1024)}, u32[]{:S(2)}) copy-start(f32[1024]{0:T(1024)} %copy-done.75) | copy-start | bytes 12292
  1423.2 79.0 %copy-start.82 = (f32[1024]{0:T(1024)S(1)}, f32[1024]{0:T(1024)}, u32[]{:S(2)}) copy-start(f32[1024]{0:T(1024)} %copy-done.81) | copy-start | bytes 12292
  1423.2 79.0 %copy-start.80 = (f32[1024]{0:T(1024)S(1)}, f32[1024]{0:T(1024)}, u32[]{:S(2)}) copy-start(f32[1024]{0:T(1024)} %copy-done.79) | copy-start | bytes 12292
  (114 other events, 1131.5 us)
Sparse Core Ops, SparseCore 0:
  16.7 60.9 all-gather.3
  318.6 126.1 reduce-scatter.4
  446.4 78.6 all-gather.5
  631.3 126.1 reduce-scatter.8
  759.9 126.1 reduce-scatter.6
  896.7 58.2 all-gather.7
  1372.6 126.1 reduce-scatter.10
  1505.4 403.8 all-reduce.6
